TPU v7x, 256 devices: a whole 4x4x8 slice. The times are simulated.
256 devices in a mesh: wide: 32 (over x, y, core), narrow: 8 (over z).
Axes of the slice: x: 4, y: 4, z: 8, core: 2. Of those that a mesh axis runs over, the one named last changes fastest.
Arguments:
- blocks: bfloat16 [32, 8, 16, 64, 4096], P('wide', 'narrow'), may hold values from -16 to 16
- row_tile: int32 [32, 8, 16], P('wide', 'narrow'), may hold values from 0 to 15
- col_tile: int32 [32, 8, 16], P('wide', 'narrow'), may hold values from 0 to 63, as said below
- depth_tile: int32 [32, 8, 16], P('wide', 'narrow'), may hold values from 0 to 15
- block_count: int32 [32, 8], P('wide', 'narrow'), may hold values from 4 to 16, as said below
- factor_b: bfloat16 [32768, 256], P(('wide', 'narrow')), may hold values from -40 to 40
- factor_c: bfloat16 [1024, 256], replicated, may hold values from -0.076293945 to 0.076293945
Outputs:
- a_new: float32 [32768, 256], P(('wide', 'narrow'))
- b_new: float32 [32768, 256], P(('wide', 'narrow'))
Inputs may be any that keep to these rules, and one draw needn't show every extreme that they name: `block_count`: every device holds at least 4 live blocks, and some device exactly 16. col_tile // 2 is the index of wide that holds the block's mode-2 factor rows; among the 16 slots of one device, live or not, each such index appears at most 1 times, and some index exactly 1 times.
All inputs are finite; a program needn't handle non-finite values.
Results may differ from a plain program's by a relative error of at most 0.02.
Values may be sent and summed in bfloat16 or wider, within the bound.
No kernel may reach another device: no remote copies, remote signals or barrier semaphores. Data moves between devices by JAX's collectives and lax.ppermute only.
A program may use at most 128 MiB of HBM per device.

v0:
```python
import jax
import jax.numpy as jnp
from jax import lax
from jax.sharding import PartitionSpec as P

TI_DEV = 2


def right_solve(target, matrix):
    chol_lower = jnp.linalg.cholesky(matrix)
    middle = lax.linalg.triangular_solve(
        chol_lower, target, left_side=False, lower=True, transpose_a=True
    )
    return lax.linalg.triangular_solve(
        chol_lower, middle, left_side=False, lower=True, transpose_a=False
    )


def column_gram(matrix):
    return lax.dot_general(
        matrix, matrix, (((0,), (0,)), ((), ())), preferred_element_type=jnp.float32
    )


def depth_mix(one_block, depth_id, factor_c, tile_rows):
    depth_rows = lax.dynamic_slice_in_dim(factor_c, depth_id * tile_rows, tile_rows, 0)
    depth_mixed = lax.dot_general(
        one_block, depth_rows, (((0,), (0,)), ((), ())), preferred_element_type=jnp.float32
    )
    return depth_mixed.reshape(tile_rows, tile_rows, depth_rows.shape[1])


def local(blocks, row_tile, col_tile, depth_tile, block_count, factor_b, factor_c):
    local_blocks = blocks[0, 0]
    first_ids = row_tile[0, 0]
    second_ids = col_tile[0, 0]
    depth_ids = depth_tile[0, 0]
    live_count = block_count[0, 0]
    tile_rows = local_blocks.shape[1]
    rank_width = factor_c.shape[1]
    wide_count = lax.axis_size("wide")
    narrow_count = lax.axis_size("narrow")
    second_local = factor_b.shape[0] // tile_rows
    owners = second_ids // second_local
    inside = second_ids % second_local
    gram_c = column_gram(factor_c)
    gram_b = lax.psum(column_gram(factor_b), ("wide", "narrow"))
    gathered = lax.all_gather(factor_b, "wide", axis=0, tiled=True)
    b_tiles = gathered.reshape(wide_count * second_local, tile_rows, rank_width)
    b_pick = owners * second_local + inside

    def first_step(slot_index, partial_sum):
        one_block = lax.dynamic_index_in_dim(local_blocks, slot_index, 0, False)
        depth_mixed = depth_mix(one_block, depth_ids[slot_index], factor_c, tile_rows)
        b_rows = lax.dynamic_index_in_dim(b_tiles, b_pick[slot_index], 0, False).astype(jnp.float32)
        b_term = jnp.sum(depth_mixed * b_rows[None, :, :], axis=1)
        target = first_ids[slot_index]
        current = lax.dynamic_index_in_dim(partial_sum, target, 0, False)
        return lax.dynamic_update_index_in_dim(partial_sum, current + b_term, target, 0)

    first_part = lax.fori_loop(
        0,
        live_count,
        first_step,
        jnp.zeros((narrow_count * TI_DEV, tile_rows, rank_width), jnp.float32),
    )
    mttkrp_a = lax.psum_scatter(
        first_part.reshape(-1, rank_width), "narrow", scatter_dimension=0, tiled=True
    )
    a_new = right_solve(mttkrp_a, gram_b * gram_c)
    a_half = a_new.astype(jnp.bfloat16)
    a_rows = lax.all_gather(a_half, "narrow", axis=0, tiled=True)
    gram_a = lax.psum(column_gram(a_half), ("wide", "narrow"))
    a_tiles = a_rows.reshape(a_rows.shape[0] // tile_rows, tile_rows, rank_width)
    width_slots = wide_count * second_local
    second_pick = owners * second_local + inside

    def second_step(slot_index, partial_sum):
        one_block = lax.dynamic_index_in_dim(local_blocks, slot_index, 0, False)
        depth_mixed = depth_mix(one_block, depth_ids[slot_index], factor_c, tile_rows)
        a_part = lax.dynamic_index_in_dim(a_tiles, first_ids[slot_index], 0, False).astype(
            jnp.float32
        )
        a_term = jnp.sum(depth_mixed * a_part[:, None, :], axis=0)
        target = second_pick[slot_index]
        current = lax.dynamic_index_in_dim(partial_sum, target, 0, False)
        return lax.dynamic_update_index_in_dim(partial_sum, current + a_term, target, 0)

    second_part = lax.fori_loop(
        0, live_count, second_step, jnp.zeros((width_slots, tile_rows, rank_width), jnp.float32)
    )
    mttkrp_b = lax.psum_scatter(
        second_part.reshape(-1, rank_width), "wide", scatter_dimension=0, tiled=True
    )
    b_new = right_solve(mttkrp_b, gram_a * gram_c)
    return (a_new, b_new)


def solution(mesh):
    return jax.shard_map(
        local,
        mesh=mesh,
        in_specs=(
            P("wide", "narrow", None, None, None),
            P("wide", "narrow", None),
            P("wide", "narrow", None),
            P("wide", "narrow", None),
            P("wide", "narrow"),
            P(("wide", "narrow"), None),
            P(),
        ),
        out_specs=(P(("wide", "narrow"), None), P(("wide", "narrow"), None)),
        check_vma=False,
    )
```

profile of v0, /device:TPU:2, one launch (start us, length us, event | category | flops | bytes accessed | tf_op | source)
XLA Modules:
  0.0 688.1 jit_solution(2137662635349681206)
XLA Ops:
  8.8 1.8 fusion.35
  10.8 15.6 %copy.22 = bf16[1,1,16,64,4096]{3,4,2,1,0:T(8,128)(2,1)} copy(bf16[1,1,16,64,4096]{4,3,2,1,0:T(8,128)(2,1)} %param.16) | data formatting | bytes 16777216 | tf_op args[0]
  26.4 36.2 %all-gather.2.cloned.1.call-done = bf16[4096,256]{1,0:T(8,128)(2,1)} async-done(((bf16[128,256]{1,0:T(8,128)(2,1)}), bf16[4096,256]{1,0:T(8,128)(2,1)}) %all-gather.2.cloned.1.call-update) | async-done | bytes 2097168 | tf_op jit(solution)/shard_map/all_gather | solution.py:48
  62.7 144.2 %while.28 = (s32[]{:T(128)}, f32[16,64,256]{2,1,0:T(8,128)S(1)}, s32[]{:T(128)}, s32[16]{0:T(128)S(1)}, bf16[16,64,4096]{1,2,0:T(8,128)(2,1)}, /*index=5*/s32[16...) while((s32[]{:T(128)}, f32[16,64,256]{2,1,0:T(8,128)S(1)}, ...), condition=%wide.region_7.9_spmd, body=%wide.region_5.8_spmd.sunk | while | flops 136331280 | bytes 2556253 | solution.py:61
  65.8 1.3 constant_dynamic-slice_fusion.8
  75.4 1.3 constant_dynamic-slice_fusion.8
  84.9 1.3 constant_dynamic-slice_fusion.8
  94.5 1.3 constant_dynamic-slice_fusion.8
  104.1 1.3 constant_dynamic-slice_fusion.8
  113.6 1.3 constant_dynamic-slice_fusion.8
  123.2 1.3 constant_dynamic-slice_fusion.8
  132.8 1.3 constant_dynamic-slice_fusion.8
  142.3 1.3 constant_dynamic-slice_fusion.8
  151.9 1.3 constant_dynamic-slice_fusion.8
  161.5 1.3 constant_dynamic-slice_fusion.8
  171.0 1.3 constant_dynamic-slice_fusion.8
  180.6 1.3 constant_dynamic-slice_fusion.8
  190.2 1.3 constant_dynamic-slice_fusion.8
  199.7 1.3 constant_dynamic-slice_fusion.8
  207.9 64.7 %all-reduce.4.cloned.1.call-done = f32[256,256]{0,1:T(8,128)} async-done(((f32[256,256]{0,1:T(8,128)}), f32[256,256]{0,1:T(8,128)}) %all-reduce.4.cloned.1.call-update) | async-done | bytes 262160 | tf_op jit(solution)/shard_map/psum | solution.py:47
  274.1 11.7 %cholesky.130 = f32[128,128]{1,0:T(8,128)S(1)} custom-call(f32[128,128]{1,0:T(8,128)S(1)} %cholesky.194), custom_call_target="Cholesky" | custom-call | tf_op jit(solution)/shard_map/jit(cholesky)/cholesky | solution.py:10
  285.9 9.8 %custom-call.17 = f32[1,128,128]{1,2,0:T(8,128)S(1)} custom-call(f32[1,128,128]{2,1,0:T(8,128)S(1)} %get-tuple-element.211), custom_call_target="InvertDiagBlocksLowerTriangular" | custom-call | tf_op jit(solution)/shard_map/jit(cholesky)/cholesky | solution.py:10
  296.2 11.7 %cholesky.147 = f32[128,128]{1,0:T(8,128)S(1)} custom-call(f32[128,128]{1,0:T(8,128)S(1)} %convolution_subtract_fusion.5), custom_call_target="Cholesky" | custom-call | tf_op jit(solution)/shard_map/jit(cholesky)/cholesky | solution.py:10
  310.0 4.2 while.30
  310.8 1.4 bitcast_dynamic-update-slice_fusion.4
  312.8 1.4 bitcast_dynamic-update-slice_fusion.4
  314.2 19.7 %custom-call.18 = f32[2,128,128]{1,2,0:T(8,128)S(1)} custom-call(f32[2,128,128]{2,1,0:T(8,128)S(1)} %get-tuple-element.131), custom_call_target="InvertDiagBlocksLowerTriangular" | custom-call | tf_op jit(solution)/shard_map/triangular_solve/custom-call.0 | solution.py:11
  337.2 24.6 %all_gather.7 = bf16[1024,256]{0,1:T(8,128)(2,1)S(1)} all-gather(bf16[128,256]{0,1:T(8,128)(2,1)S(1)} %fusion.31), channel_id=1, replica_groups=mesh['wide'=32,'narrow'=8] {'narrow'}, dimensions={0}, use_global_device_ids=true | all-gather | bytes 589824 | tf_op jit(solution)/shard_map/all_gather | solution.py:72
  362.9 2.4 broadcast_in_dim.14
  365.4 159.6 %while.29 = (s32[]{:T(128)}, f32[64,64,256]{2,1,0:T(8,128)}, s32[]{:T(128)}, s32[16]{0:T(128)S(1)}, bf16[16,64,4096]{1,2,0:T(8,128)(2,1)}, /*index=5*/s32[16]{0:...) while((s32[]{:T(128)}, f32[64,64,256]{2,1,0:T(8,128)}, ...), condition=%wide.region_12.16_spmd, body=%wide.region_10.15_spmd.sunk | while | flops 136331280 | bytes 2556253 | solution.py:89
  368.6 1.3 constant_dynamic-slice_fusion.9
  374.5 1.5 fusion.72
  379.2 1.3 constant_dynamic-slice_fusion.9
  385.1 1.5 fusion.72
  389.7 1.3 constant_dynamic-slice_fusion.9
  395.7 1.5 fusion.72
  400.3 1.3 constant_dynamic-slice_fusion.9
  406.3 1.5 fusion.72
  410.9 1.3 constant_dynamic-slice_fusion.9
  416.9 1.5 fusion.72
  421.5 1.3 constant_dynamic-slice_fusion.9
  427.5 1.5 fusion.72
  432.1 1.3 constant_dynamic-slice_fusion.9
  438.1 1.5 fusion.72
  448.6 1.5 fusion.72
  453.3 1.3 constant_dynamic-slice_fusion.9
  459.2 1.5 fusion.72
  469.8 1.5 fusion.72
  474.5 1.3 constant_dynamic-slice_fusion.9
  480.4 1.5 fusion.72
  491.0 1.5 fusion.72
  495.7 1.3 constant_dynamic-slice_fusion.9
  501.6 1.5 fusion.72
  506.3 1.3 constant_dynamic-slice_fusion.9
  512.2 1.5 fusion.72
  522.8 1.5 fusion.72
  525.7 89.8 %all-reduce.6.cloned.1.call-done = f32[256,256]{0,1:T(8,128)} async-done(((f32[256,256]{0,1:T(8,128)}), f32[256,256]{0,1:T(8,128)}) %all-reduce.6.cloned.1.call-update) | async-done | bytes 262160 | tf_op jit(solution)/shard_map/psum | solution.py:73
  616.7 11.7 %cholesky.164 = f32[128,128]{1,0:T(8,128)S(1)} custom-call(f32[128,128]{1,0:T(8,128)S(1)} %cholesky.197), custom_call_target="Cholesky" | custom-call | tf_op jit(solution)/shard_map/jit(cholesky)/cholesky | solution.py:10
  628.5 9.8 %custom-call.20 = f32[1,128,128]{1,2,0:T(8,128)S(1)} custom-call(f32[1,128,128]{2,1,0:T(8,128)S(1)} %get-tuple-element.207), custom_call_target="InvertDiagBlocksLowerTriangular" | custom-call | tf_op jit(solution)/shard_map/jit(cholesky)/cholesky | solution.py:10
  638.7 11.7 %cholesky.181 = f32[128,128]{1,0:T(8,128)S(1)} custom-call(f32[128,128]{1,0:T(8,128)S(1)} %convolution_subtract_fusion.2), custom_call_target="Cholesky" | custom-call | tf_op jit(solution)/shard_map/jit(cholesky)/cholesky | solution.py:10
  653.1 4.1 while.31
  654.0 1.3 bitcast_dynamic-update-slice_fusion.5
  655.9 1.3 bitcast_dynamic-update-slice_fusion.5
  657.3 19.7 %custom-call.21 = f32[2,128,128]{1,2,0:T(8,128)S(1)} custom-call(f32[2,128,128]{2,1,0:T(8,128)S(1)} %get-tuple-element.133), custom_call_target="InvertDiagBlocksLowerTriangular" | custom-call | tf_op jit(solution)/shard_map/triangular_solve/custom-call.0 | solution.py:11
  (247 shorter events, 112.4 us)
Async XLA Ops:
  8.0 54.6 %all-gather.2.cloned.1.call-start = ((), (), s32[]{:S(2)}) async-start(), calls=%async_computation.3 | async-start | bytes 2162688 | tf_op jit(solution)/shard_map/all_gather | solution.py:48
  8.7 263.9 %all-reduce.4.cloned.1.call-start = ((), (), s32[]{:S(2)}) async-start(), calls=%async_computation.2 | async-start | bytes 524288 | tf_op jit(solution)/shard_map/psum | solution.py:47
  10.7 323.2 %reduce-scatter.3.cloned.1.call-start = ((), (), s32[]{:S(2)}) async-start(), calls=%async_computation.4 | async-start | bytes 1179648 | tf_op jit(solution)/shard_map/reduce_scatter | solution.py:67
  10.7 15.7 %copy-start.2 = (s32[1,1,16]{2,1,0:T(1,128)S(1)}, s32[1,1,16]{2,1,0:T(1,128)}, u32[]{:S(2)}) copy-start(s32[1,1,16]{2,1,0:T(1,128)} %param.18) | copy-start | bytes 196
  10.7 51.9 %copy-start.1 = (bf16[1024,256]{1,0:T(8,128)(2,1)S(1)}, bf16[1024,256]{1,0:T(8,128)(2,1)}, u32[]{:S(2)}) copy-start(bf16[1024,256]{1,0:T(8,128)(2,1)} %param.22) | copy-start | bytes 1572868
  10.7 51.9 %copy-start.3 = (s32[1,1,16]{2,1,0:T(1,128)S(1)}, s32[1,1,16]{2,1,0:T(1,128)}, u32[]{:S(2)}) copy-start(s32[1,1,16]{2,1,0:T(1,128)} %param.17) | copy-start | bytes 196
  10.7 51.9 %copy-start.4 = (s32[1,1,16]{2,1,0:T(1,128)S(1)}, s32[1,1,16]{2,1,0:T(1,128)}, u32[]{:S(2)}) copy-start(s32[1,1,16]{2,1,0:T(1,128)} %param.19) | copy-start | bytes 196
  206.9 1.0 copy-start
  207.9 407.6 %all-reduce.6.cloned.1.call-start = ((), (), s32[]{:S(2)}) async-start(), calls=%async_computation.5 | async-start | bytes 524288 | tf_op jit(solution)/shard_map/psum | solution.py:73
  362.9 314.1 %reduce-scatter.5.cloned.1.call-start = ((), (), s32[]{:S(2)}) async-start(), calls=%async_computation.6 | async-start | bytes 4325376 | tf_op jit(solution)/shard_map/reduce_scatter | solution.py:92
Sparse Core Ops, SparseCore 0:
  11.4 51.1 all-gather.1
  208.0 42.8 reduce-scatter.2
  525.1 93.6 reduce-scatter.4
Sparse Core Ops, SparseCore 1:
  14.7 257.9 all-reduce.3
  363.0 252.5 all-reduce.5
where the time goes:
time: 694 us; the launch traced here: 688 us
  waiting for transfers between devices  191 us (28%)
  loops' own time  155 us (22%)
  other arithmetic  143 us (21%)
  local copies, waits for them, and re-layouts  121 us (17%)
  matrix products  34.1 us (5%)
  blocking collectives  24.6 us (4%)
  between operations  18.1 us (3%)
    psum x1, waiting for transfers between devices, local(): gram_a = lax.psum(column_gram(a_half), ('wide', 'narrow'))  89.8 us
    another operation x1, loops' own time, local(): lax.fori_loop(0, live_count, second_step, jnp.zeros((width_slots, tile_ro...  79.1 us
    another operation x1, loops' own time, local(): lax.fori_loop(0, live_count, first_step, jnp.zeros((narrow_count * TI_DEV...  75.7 us
    another operation x13, other arithmetic, right_solve(): chol_lower = jnp.linalg.cholesky(matrix)  68.6 us
    psum x1, waiting for transfers between devices, local(): gram_b = lax.psum(column_gram(factor_b), ('wide', 'narrow'))  64.7 us
    another operation x5, other arithmetic, right_solve(): lax.linalg.triangular_solve(chol_lower, target, left_side=False, lower=Tr...  39.4 us
    all_gather x1, waiting for transfers between devices, local(): gathered = lax.all_gather(factor_b, 'wide', axis=0, tiled=True)  36.2 us
    all_gather x1, blocking collectives, local(): a_rows = lax.all_gather(a_half, 'narrow', axis=0, tiled=True)  24.6 us
  transfers between devices with their start and end apart: 5, of which 3 were waited for; matrix products, arithmetic and copies ran while one was open for 42% of the time, Pallas kernels for 0%

commit v1 on v0

--- a/solution.py
+++ b/solution.py
@@ -70,7 +70,7 @@
     a_new = right_solve(mttkrp_a, gram_b * gram_c)
     a_half = a_new.astype(jnp.bfloat16)
     a_rows = lax.all_gather(a_half, "narrow", axis=0, tiled=True)
-    gram_a = lax.psum(column_gram(a_half), ("wide", "narrow"))
+    gram_a = jnp.sum(lax.all_gather(column_gram(a_half), ("wide", "narrow")), axis=0)
     a_tiles = a_rows.reshape(a_rows.shape[0] // tile_rows, tile_rows, rank_width)
     width_slots = wide_count * second_local
     second_pick = owners * second_local + inside

time: 694 us -> 651 us (0.938)
  waiting for transfers between devices: 191 us -> 131 us
  other arithmetic: 143 us -> 165 us
  loops' own time: 155 us -> 147 us
    psum x1 -> x0, waiting for transfers between devices: 89.8 us -> none  [local(): gram_a = lax.psum(column_gram(a_half), ('wide', 'narrow'))]
    all_gather x0 -> x1, waiting for transfers between devices: none -> 33.6 us  [local(): lax.all_gather(column_gram(a_half), ('wide', 'narrow'))]
    reduce_sum x0 -> x1, other arithmetic: none -> 22.1 us  [local(): jnp.sum(lax.all_gather(column_gram(a_half), ('wide', 'narrow')), axis=0)]
    another operation x1, loops' own time: 79.1 us -> 68.5 us  [local(): lax.fori_loop(0, live_count, second_step, jnp.zeros((width_slots, tile_ro...]
  transfers between devices with their start and end apart: 5 -> 5, of which waited for: 3 -> 3; matrix products, arithmetic and copies ran while one was open for 42% -> 49% of each run, Pallas kernels for 0% -> 0%
where the time goes in v1:
time: 651 us; the launch traced here: 644 us
  other arithmetic  165 us (25%)
  loops' own time  147 us (23%)
  waiting for transfers between devices  131 us (20%)
  local copies, waits for them, and re-layouts  123 us (19%)
  matrix products  34.1 us (5%)
  blocking collectives  25.7 us (4%)
  between operations  18.1 us (3%)
    another operation x1, loops' own time, local(): lax.fori_loop(0, live_count, first_step, jnp.zeros((narrow_count * TI_DEV...  77.8 us
    another operation x13, other arithmetic, right_solve(): chol_lower = jnp.linalg.cholesky(matrix)  68.7 us
    another operation x1, loops' own time, local(): lax.fori_loop(0, live_count, second_step, jnp.zeros((width_slots, tile_ro...  68.5 us
    psum x1, waiting for transfers between devices, local(): gram_b = lax.psum(column_gram(factor_b), ('wide', 'narrow'))  60.4 us
    another operation x5, other arithmetic, right_solve(): lax.linalg.triangular_solve(chol_lower, target, left_side=False, lower=Tr...  39.6 us
    all_gather x1, waiting for transfers between devices, local(): gathered = lax.all_gather(factor_b, 'wide', axis=0, tiled=True)  36.2 us
    all_gather x1, waiting for transfers between devices, local(): lax.all_gather(column_gram(a_half), ('wide', 'narrow'))  33.6 us
    all_gather x1, blocking collectives, local(): a_rows = lax.all_gather(a_half, 'narrow', axis=0, tiled=True)  25.7 us
  transfers between devices with their start and end apart: 5, of which 3 were waited for; matrix products, arithmetic and copies ran while one was open for 49% of the time, Pallas kernels for 0%

profile of v1, /device:TPU:2, one launch (start us, length us, event | category | flops | bytes accessed | tf_op | source)
XLA Modules:
  0.0 643.7 jit_solution(4741939585253606918)
XLA Ops:
  8.8 1.8 fusion.35
  10.8 15.6 %copy.30 = bf16[1,1,16,64,4096]{3,4,2,1,0:T(8,128)(2,1)} copy(bf16[1,1,16,64,4096]{4,3,2,1,0:T(8,128)(2,1)} %param.16) | data formatting | bytes 16777216 | tf_op args[0]
  26.3 36.2 %all-gather.4.cloned.1.call-done = bf16[4096,256]{1,0:T(8,128)(2,1)} async-done(((bf16[128,256]{1,0:T(8,128)(2,1)}), bf16[4096,256]{1,0:T(8,128)(2,1)}) %all-gather.4.cloned.1.call-update) | async-done | bytes 2097168 | tf_op jit(solution)/shard_map/all_gather | solution.py:48
  62.7 148.9 %while.28 = (s32[]{:T(128)}, f32[16,64,256]{2,1,0:T(8,128)S(1)}, s32[]{:T(128)}, s32[16]{0:T(128)S(1)}, bf16[16,64,4096]{1,2,0:T(8,128)(2,1)}, /*index=5*/s32[16...) while((s32[]{:T(128)}, f32[16,64,256]{2,1,0:T(8,128)S(1)}, ...), condition=%wide.region_7.9_spmd, body=%wide.region_5.8_spmd.sunk | while | flops 136331280 | bytes 2556253 | solution.py:61
  65.9 1.3 constant_dynamic-slice_fusion.8
  75.8 1.3 constant_dynamic-slice_fusion.8
  85.7 1.3 constant_dynamic-slice_fusion.8
  95.6 1.3 constant_dynamic-slice_fusion.8
  105.5 1.3 constant_dynamic-slice_fusion.8
  115.3 1.3 constant_dynamic-slice_fusion.8
  125.2 1.3 constant_dynamic-slice_fusion.8
  135.1 1.3 constant_dynamic-slice_fusion.8
  145.0 1.3 constant_dynamic-slice_fusion.8
  154.9 1.3 constant_dynamic-slice_fusion.8
  164.8 1.3 constant_dynamic-slice_fusion.8
  184.5 1.3 constant_dynamic-slice_fusion.8
  194.4 1.3 constant_dynamic-slice_fusion.8
  204.3 1.3 constant_dynamic-slice_fusion.8
  212.7 60.4 %all-reduce.3.cloned.1.call-done = f32[256,256]{0,1:T(8,128)} async-done(((f32[256,256]{0,1:T(8,128)}), f32[256,256]{0,1:T(8,128)}) %all-reduce.3.cloned.1.call-update) | async-done | bytes 262160 | tf_op jit(solution)/shard_map/psum | solution.py:47
  274.6 11.7 %cholesky.130 = f32[128,128]{1,0:T(8,128)S(1)} custom-call(f32[128,128]{1,0:T(8,128)S(1)} %cholesky.194), custom_call_target="Cholesky" | custom-call | tf_op jit(solution)/shard_map/jit(cholesky)/cholesky | solution.py:10
  286.4 9.8 %custom-call.17 = f32[1,128,128]{1,2,0:T(8,128)S(1)} custom-call(f32[1,128,128]{2,1,0:T(8,128)S(1)} %get-tuple-element.213), custom_call_target="InvertDiagBlocksLowerTriangular" | custom-call | tf_op jit(solution)/shard_map/jit(cholesky)/cholesky | solution.py:10
  296.7 11.7 %cholesky.147 = f32[128,128]{1,0:T(8,128)S(1)} custom-call(f32[128,128]{1,0:T(8,128)S(1)} %convolution_subtract_fusion.5), custom_call_target="Cholesky" | custom-call | tf_op jit(solution)/shard_map/jit(cholesky)/cholesky | solution.py:10
  310.5 4.1 while.30
  311.3 1.4 bitcast_dynamic-update-slice_fusion.4
  313.3 1.4 bitcast_dynamic-update-slice_fusion.4
  314.7 19.7 %custom-call.18 = f32[2,128,128]{1,2,0:T(8,128)S(1)} custom-call(f32[2,128,128]{2,1,0:T(8,128)S(1)} %get-tuple-element.131), custom_call_target="InvertDiagBlocksLowerTriangular" | custom-call | tf_op jit(solution)/shard_map/triangular_solve/custom-call.0 | solution.py:11
  338.6 25.7 %all_gather.15 = bf16[1024,256]{0,1:T(8,128)(2,1)S(1)} all-gather(bf16[128,256]{0,1:T(8,128)(2,1)S(1)} %fusion.31), channel_id=1, replica_groups=mesh['wide'=32,'narrow'=8] {'narrow'}, dimensions={0}, use_global_device_ids=true | all-gather | bytes 589824 | tf_op jit(solution)/shard_map/all_gather | solution.py:72
  364.6 2.5 broadcast_in_dim.14
  367.0 148.2 %while.29 = (s32[]{:T(128)}, f32[64,64,256]{2,1,0:T(8,128)}, s32[]{:T(128)}, s32[16]{0:T(128)S(1)}, bf16[16,64,4096]{1,2,0:T(8,128)(2,1)}, /*index=5*/s32[16]{0:...) while((s32[]{:T(128)}, f32[64,64,256]{2,1,0:T(8,128)}, ...), condition=%wide.region_12.16_spmd, body=%wide.region_10.15_spmd.sunk | while | flops 136331280 | bytes 2556253 | solution.py:89
  369.9 1.3 constant_dynamic-slice_fusion.9
  375.3 1.5 fusion.72
  379.7 1.3 constant_dynamic-slice_fusion.9
  385.1 1.5 fusion.72
  394.9 1.5 fusion.72
  399.3 1.3 constant_dynamic-slice_fusion.9
  404.7 1.5 fusion.72
  409.1 1.3 constant_dynamic-slice_fusion.9
  414.5 1.5 fusion.72
  418.9 1.3 constant_dynamic-slice_fusion.9
  424.3 1.5 fusion.72
  434.1 1.5 fusion.72
  444.0 1.5 fusion.72
  448.3 1.3 constant_dynamic-slice_fusion.9
  453.7 1.5 fusion.72
  458.1 1.4 constant_dynamic-slice_fusion.9
  463.6 1.5 fusion.72
  468.0 1.5 constant_dynamic-slice_fusion.9
  473.6 1.5 fusion.72
  477.9 1.3 constant_dynamic-slice_fusion.9
  483.4 1.5 fusion.72
  487.8 1.4 constant_dynamic-slice_fusion.9
  493.4 1.5 fusion.72
  497.7 1.4 constant_dynamic-slice_fusion.9
  503.3 1.5 fusion.72
  513.1 1.5 fusion.72
  516.0 33.6 %all-gather.6.cloned.1.call-done = f32[65536,256]{1,0:T(8,128)} async-done(((f32[256,256]{1,0:T(8,128)}), f32[65536,256]{1,0:T(8,128)}) %all-gather.6.cloned.1.call-update) | async-done | bytes 67108880 | tf_op jit(solution)/shard_map/all_gather | solution.py:73
  549.6 22.1 %reduce_sum.31 = f32[256,256]{1,0:T(8,128)S(1)} reduce(f32[256,256,256]{2,1,0:T(8,128)} %bitcast.34, f32[]{:T(128)} %constant.146.clone.1), dimensions={0}, to_apply=%region_9.13 | reduce | flops 16711680 | bytes 67371008 | tf_op jit(solution)/shard_map/reduce_sum | solution.py:73
  572.1 11.7 %cholesky.164 = f32[128,128]{1,0:T(8,128)S(1)} custom-call(f32[128,128]{1,0:T(8,128)S(1)} %cholesky.197), custom_call_target="Cholesky" | custom-call | tf_op jit(solution)/shard_map/jit(cholesky)/cholesky | solution.py:10
  583.8 9.8 %custom-call.20 = f32[1,128,128]{1,2,0:T(8,128)S(1)} custom-call(f32[1,128,128]{2,1,0:T(8,128)S(1)} %get-tuple-element.209), custom_call_target="InvertDiagBlocksLowerTriangular" | custom-call | tf_op jit(solution)/shard_map/jit(cholesky)/cholesky | solution.py:10
  594.1 11.7 %cholesky.181 = f32[128,128]{1,0:T(8,128)S(1)} custom-call(f32[128,128]{1,0:T(8,128)S(1)} %convolution_subtract_fusion.2), custom_call_target="Cholesky" | custom-call | tf_op jit(solution)/shard_map/jit(cholesky)/cholesky | solution.py:10
  608.5 4.1 while.31
  609.2 1.3 bitcast_dynamic-update-slice_fusion.5
  611.3 1.3 bitcast_dynamic-update-slice_fusion.5
  612.6 19.9 %custom-call.21 = f32[2,128,128]{1,2,0:T(8,128)S(1)} custom-call(f32[2,128,128]{2,1,0:T(8,128)S(1)} %get-tuple-element.133), custom_call_target="InvertDiagBlocksLowerTriangular" | custom-call | tf_op jit(solution)/shard_map/triangular_solve/custom-call.0 | solution.py:11
  (249 shorter events, 114.3 us)
Async XLA Ops:
  8.0 54.6 %all-gather.4.cloned.1.call-start = ((), (), s32[]{:S(2)}) async-start(), calls=%async_computation.3 | async-start | bytes 2162688 | tf_op jit(solution)/shard_map/all_gather | solution.py:48
  8.7 264.4 %all-reduce.3.cloned.1.call-start = ((), (), s32[]{:S(2)}) async-start(), calls=%async_computation.2 | async-start | bytes 524288 | tf_op jit(solution)/shard_map/psum | solution.py:47
  10.7 323.7 %reduce-scatter.3.cloned.1.call-start = ((), (), s32[]{:S(2)}) async-start(), calls=%async_computation.4 | async-start | bytes 1179648 | tf_op jit(solution)/shard_map/reduce_scatter | solution.py:67
  10.7 15.6 %copy-start.2 = (s32[1,1,16]{2,1,0:T(1,128)S(1)}, s32[1,1,16]{2,1,0:T(1,128)}, u32[]{:S(2)}) copy-start(s32[1,1,16]{2,1,0:T(1,128)} %param.18) | copy-start | bytes 196
  10.7 52.0 %copy-start.1 = (bf16[1024,256]{1,0:T(8,128)(2,1)S(1)}, bf16[1024,256]{1,0:T(8,128)(2,1)}, u32[]{:S(2)}) copy-start(bf16[1024,256]{1,0:T(8,128)(2,1)} %param.22) | copy-start | bytes 1572868
  10.7 51.9 %copy-start.3 = (s32[1,1,16]{2,1,0:T(1,128)S(1)}, s32[1,1,16]{2,1,0:T(1,128)}, u32[]{:S(2)}) copy-start(s32[1,1,16]{2,1,0:T(1,128)} %param.17) | copy-start | bytes 196
  10.7 51.9 %copy-start.4 = (s32[1,1,16]{2,1,0:T(1,128)S(1)}, s32[1,1,16]{2,1,0:T(1,128)}, u32[]{:S(2)}) copy-start(s32[1,1,16]{2,1,0:T(1,128)} %param.19) | copy-start | bytes 196
  211.6 1.0 copy-start
  212.6 336.9 %all-gather.6.cloned.1.call-start = ((), (), s32[]{:S(2)}) async-start(), calls=%async_computation.6 | async-start | bytes 67371008 | tf_op jit(solution)/shard_map/all_gather | solution.py:73
  338.6 294.0 %reduce-scatter.5.cloned.1.call-start = ((), (), s32[]{:S(2)}) async-start(), calls=%async_computation.5 | async-start | bytes 4325376 | tf_op jit(solution)/shard_map/reduce_scatter | solution.py:92
Sparse Core Ops, SparseCore 0:
  11.4 51.1 all-gather.3
  212.7 43.1 reduce-scatter.2
  515.4 98.8 reduce-scatter.4
Sparse Core Ops, SparseCore 1:
  14.7 258.4 all-reduce.2
  338.7 210.9 all-gather.5
